TPU v7x, 512 devices: a whole 4x8x8 slice. The times are simulated.
512 devices in a mesh: row: 32 (over z, x_lo, core), col: 16 (over x_hi, y).
Axes of the slice: x: 4 (x_hi: 2, x_lo: 2; x = x_hi * 2 + x_lo), y: 8, z: 8, core: 2. Of those that a mesh axis runs over, the one named last changes fastest.
Arguments:
- slab_block: bfloat16 [65536, 2048], P('row', 'col'), may hold values from -6 to 6
- scale_first: bfloat16 [65536], P('row'), may hold values from 0.5 to 2
- scale_second: bfloat16 [65536], P('row'), may hold values from 0.5 to 2
- panel_lower: bfloat16 [65536, 4096], P('row', 'col'), may hold values from -0.09375 to 0.09375
Outputs:
- updated_slab: bfloat16 [65536, 2048], P('row', 'col')
All inputs are finite; a program needn't handle non-finite values.
Results may differ from a plain program's by a relative error of at most 0.015.
Values may be sent and summed in bfloat16 or wider, within the bound.
No kernel may reach another device: no remote copies, remote signals or barrier semaphores. Data moves between devices by JAX's collectives and lax.ppermute only.
A program may use at most 64 MiB of HBM per device.

v0:
```python
import jax
import jax.numpy as jnp
from jax import lax
from jax.sharding import PartitionSpec as P

PANEL_W = 4096
inv_root = 0.7071067811865476


def from_partner(block, axis, bit):
    count = lax.axis_size(axis)
    route = []
    for low in range(count):
        high = low | 1 << bit
        if high != low and high < count:
            route += [(low, high), (high, low)]
    return lax.ppermute(block, axis, route)


def per_device(slab_block, scale_first, scale_second, panel_lower):
    row_count, col_width = slab_block.shape
    groups = lax.axis_size("row")
    top_bit = groups.bit_length() - 1
    first = (scale_first.astype(jnp.float32)[:, None] * slab_block.astype(jnp.float32)).astype(
        jnp.bfloat16
    )
    my_index = lax.axis_index("row")
    partner = from_partner(first, "row", top_bit - 1)
    upper_one = my_index // (groups // 2) % 2 == 0
    own_vals = first.astype(jnp.float32)
    far_vals = partner.astype(jnp.float32)
    level_one = jnp.where(
        upper_one, (own_vals + far_vals) * inv_root, (far_vals - own_vals) * inv_root
    )
    second = (scale_second.astype(jnp.float32)[:, None] * level_one).astype(jnp.bfloat16)
    partner_two = from_partner(second, "row", top_bit - 2)
    upper_two = my_index // (groups // 4) % 2 == 0
    own_two = second.astype(jnp.float32)
    far_two = partner_two.astype(jnp.float32)
    level_two = jnp.where(upper_two, (own_two + far_two) * inv_root, (far_two - own_two) * inv_root)
    transformed = level_two.astype(jnp.bfloat16)
    moved = lax.all_to_all(
        transformed.reshape(row_count // groups, groups, col_width),
        "row",
        split_axis=1,
        concat_axis=0,
        tiled=True,
    )
    stored = moved.reshape(row_count, col_width)
    top_count = PANEL_W // groups
    top_local = stored[:top_count].reshape(top_count, 1, col_width)
    upper_rows = lax.all_gather(top_local, "row", axis=1, tiled=True).reshape(PANEL_W, col_width)
    block_width = panel_lower.shape[1]
    empty_sum = jnp.zeros((row_count, col_width), jnp.float32)
    shard_piece = lax.all_gather(panel_lower, "col", axis=1, tiled=True)
    blocks_in = shard_piece.shape[1] // block_width

    def one_block(blocknum, running):
        panel_part = lax.dynamic_slice_in_dim(shard_piece, blocknum * block_width, block_width, 1)
        rows_used = lax.dynamic_slice_in_dim(upper_rows, blocknum * block_width, block_width, 0)
        product = jnp.dot(panel_part, rows_used, preferred_element_type=jnp.float32)
        return running + product.astype(jnp.bfloat16).astype(jnp.float32)

    update_sum = lax.fori_loop(0, blocks_in, one_block, empty_sum)
    return (stored.astype(jnp.float32) - update_sum).astype(jnp.bfloat16)


def solution(mesh):
    placed = (P("row", "col"), P("row"), P("row"), P("row", "col"))
    return jax.shard_map(
        per_device, mesh=mesh, in_specs=placed, out_specs=P("row", "col"), check_vma=False
    )
```

profile of v0, /device:TPU:8, one launch (start us, length us, event | category | flops | bytes accessed | tf_op | source)
XLA Modules:
  0.0 444.3 jit_solution(17364804723847924911)
XLA Ops:
  6.5 0.0 all-gather.5.cloned.1.call-start
  6.5 0.7 convert_element_type.54
  7.2 1.4 multiply_convert_fusion
  8.6 10.9 %collective-permute-start = (bf16[2048,128]{1,0:T(8,128)(2,1)S(1)}, bf16[2048,128]{1,0:T(8,128)(2,1)S(1)}, u32[]{:S(2)}, u32[]{:S(2)}) collective-permute-start(bf16[2048,128]{1,0:T(8,128)(2,1)S(1)} %multiply_convert_fusion), channel_id=1, source_target_pairs={{0,256},{256,0},{16,272},{272,16},{32,288},{288,32},{48,304},{304,... | collective-permute-start | bytes 1572872 | tf_op jit(solution)/shard_map/ppermute | solution.py:17
  19.6 0.7 convert_element_type.53
  20.3 11.4 %collective-permute-done = bf16[2048,128]{1,0:T(8,128)(2,1)S(1)} collective-permute-done((bf16[2048,128]{1,0:T(8,128)(2,1)S(1)}, bf16[2048,128]{1,0:T(8,128)(2,1)S(1)}, u32[]{:S(2)}, u32[]{:S(2)}) %collective-permute-start) | collective-permute-done | bytes 524320 | tf_op jit(solution)/shard_map/ppermute | solution.py:17
  31.6 1.7 fusion.8
  33.3 15.4 %collective-permute-start.1 = (bf16[2048,128]{1,0:T(8,128)(2,1)S(1)}, bf16[2048,128]{1,0:T(8,128)(2,1)S(1)}, u32[]{:S(2)}, u32[]{:S(2)}) collective-permute-start(bf16[2048,128]{1,0:T(8,128)(2,1)S(1)} %fusion.8), channel_id=1, source_target_pairs={{0,128},{128,0},{16,144},{144,16},{32,160},{160,32},{48,176},{176,... | collective-permute-start | bytes 1572872 | tf_op jit(solution)/shard_map/ppermute | solution.py:17
  48.7 23.2 %collective-permute-done.1 = bf16[2048,128]{1,0:T(8,128)(2,1)S(1)} collective-permute-done((bf16[2048,128]{1,0:T(8,128)(2,1)S(1)}, bf16[2048,128]{1,0:T(8,128)(2,1)S(1)}, u32[]{:S(2)}, u32[]{:S(2)}) %collective-permute-start.1) | collective-permute-done | bytes 524320 | tf_op jit(solution)/shard_map/ppermute | solution.py:17
  72.0 0.3 fusion.12
  72.2 0.2 copy.8
  72.4 25.9 %all_to_all.15 = bf16[64,32,128]{2,0,1:T(8,128)(2,1)S(1)} all-to-all(bf16[64,32,128]{2,0,1:T(8,128)(2,1)S(1)} %copy.8), channel_id=1, replica_groups=mesh['row'=32,'col'=16] {'row'}, dimensions={1} | all-to-all | bytes 1048576 | tf_op jit(solution)/shard_map/all_to_all | solution.py:42
  98.3 0.6 slice.5
  99.0 0.0 all-gather.5.cloned.1.call-update
  99.0 0.0 all-gather.3.cloned.1.call-start
  99.0 0.7 all-gather.3.cloned.1.call-update
  99.7 62.5 %all-gather.5.cloned.1.call-done = bf16[128,32,128]{2,0,1:T(8,128)(2,1)} async-done(((bf16[128,1,128]{2,0,1:T(8,128)(2,1)}), bf16[128,32,128]{2,0,1:T(8,128)(2,1)}) %all-gather.5.cloned.1.call-update) | async-done | bytes 1048592 | tf_op jit(solution)/shard_map/all_gather | solution.py:52
  162.2 1.9 copy.9
  164.1 243.9 %all-gather.3.cloned.1.call-done = bf16[2048,4096]{1,0:T(8,128)(2,1)} async-done(((bf16[2048,256]{1,0:T(8,128)(2,1)}), bf16[2048,4096]{1,0:T(8,128)(2,1)}) %all-gather.3.cloned.1.call-update) | async-done | bytes 16777232 | tf_op jit(solution)/shard_map/all_gather | solution.py:55
  408.0 28.6 %while.14 = (s32[]{:T(128)}, f32[2048,128]{1,0:T(8,128)S(1)}, bf16[2048,4096]{1,0:T(8,128)(2,1)}, bf16[4096,128]{1,0:T(8,128)(2,1)S(1)}, s32[]{:T(128)}, /*index=5*/s32[]{:T(128)}, s32[]{:T(128)}, s32[]{:T(128)}) while((s32[]{:T(128)}, f32[2048,128]{1,0:T(8,128)S(1)}, bf16[2048,4096]{1,0:T(8,128)(2,1)}, ...), condition=%wide.region_1.2_spmd.clone, body=%wide.region_0.1_spmd.clone.sunk | while | flops 135266304 | bytes 3212948 | solution.py:64
  408.0 1.8 fusion.20
  409.8 1.8 fusion.20
  411.6 1.8 fusion.20
  413.3 1.8 fusion.20
  415.1 1.8 fusion.20
  416.9 1.8 fusion.20
  418.7 1.8 fusion.20
  420.5 1.8 fusion.20
  422.3 1.8 fusion.20
  424.1 1.8 fusion.20
  425.9 1.8 fusion.20
  427.6 1.8 fusion.20
  429.4 1.8 fusion.20
  431.2 1.8 fusion.20
  433.0 1.8 fusion.20
  434.8 1.8 fusion.20
  436.6 0.9 fusion.14
  (1 shorter events, 0.0 us)
Async XLA Ops:
  6.5 155.7 %all-gather.5.cloned.1.call-start = ((), (), s32[]{:S(2)}) async-start(), calls=%async_computation.2 | async-start | bytes 1081344 | tf_op jit(solution)/shard_map/all_gather | solution.py:52
  8.6 23.0 %collective-permute-start = (bf16[2048,128]{1,0:T(8,128)(2,1)S(1)}, bf16[2048,128]{1,0:T(8,128)(2,1)S(1)}, u32[]{:S(2)}, u32[]{:S(2)}) collective-permute-start(bf16[2048,128]{1,0:T(8,128)(2,1)S(1)} %multiply_convert_fusion), channel_id=1, source_target_pairs={{0,256},{256,0},{16,272},{272,16},{32,288},{288,32},{48,304},{304,... | collective-permute-start | bytes 1572872 | tf_op jit(solution)/shard_map/ppermute | solution.py:17
  33.3 38.7 %collective-permute-start.1 = (bf16[2048,128]{1,0:T(8,128)(2,1)S(1)}, bf16[2048,128]{1,0:T(8,128)(2,1)S(1)}, u32[]{:S(2)}, u32[]{:S(2)}) collective-permute-start(bf16[2048,128]{1,0:T(8,128)(2,1)S(1)} %fusion.8), channel_id=1, source_target_pairs={{0,128},{128,0},{16,144},{144,16},{32,160},{160,32},{48,176},{176,... | collective-permute-start | bytes 1572872 | tf_op jit(solution)/shard_map/ppermute | solution.py:17
  99.0 309.0 %all-gather.3.cloned.1.call-start = ((), (), s32[]{:S(2)}) async-start(), calls=%async_computation.1 | async-start | bytes 17825792 | tf_op jit(solution)/shard_map/all_gather | solution.py:55
Sparse Core Ops, SparseCore 0:
  99.1 63.0 all-gather.4
  165.3 242.6 all-gather.2
where the time goes:
time: 445 us; the launch traced here: 444 us
  waiting for transfers between devices  342 us (77%)
  matrix products  28.1 us (6%)
  starting transfers between devices  26.4 us (6%)
  blocking collectives  25.9 us (6%)
  between operations  13.5 us (3%)
  other arithmetic  5.61 us (1%)
    all_gather x1, waiting for transfers between devices, per_device(): shard_piece = lax.all_gather(panel_lower, 'col', axis=1, tiled=True)  244 us
    all_gather x1, waiting for transfers between devices, per_device(): lax.all_gather(top_local, 'row', axis=1, tiled=True)  62.5 us
    ppermute x2, waiting for transfers between devices, from_partner(): return lax.ppermute(block, axis, route)  34.6 us
    dot_general x16, matrix products, one_block(): product = jnp.dot(panel_part, rows_used, preferred_element_type=jnp.float32)  28.1 us
    ppermute x2, starting transfers between devices, from_partner(): return lax.ppermute(block, axis, route)  26.4 us
    all_to_all x1, blocking collectives, per_device(): lax.all_to_all(transformed.reshape(row_count // groups, groups, col_width...  25.9 us
  transfers between devices with their start and end apart: 4, of which 4 were waited for; matrix products, arithmetic and copies ran while one was open for 1% of the time, Pallas kernels for 0%

commit v1 on v0

--- a/solution.py
+++ b/solution.py
@@ -1,3 +1,4 @@
+import functools
 import jax
 import jax.numpy as jnp
 from jax import lax
@@ -5,6 +6,15 @@
 
 PANEL_W = 4096
 inv_root = 0.7071067811865476
+
+
+def divide_joints(row_data, d0):
+    carry_out = jnp.stack(lax.axis_size("col") * [row_data], 0)
+    block_now = lax.all_to_all(carry_out, "col", 0, 0)
+    return jnp.concatenate(block_now, d0)
+
+
+arrange_the_shifts_all = functools.partial(divide_joints, d0=1)
 
 
 def from_partner(block, axis, bit):
@@ -52,7 +62,7 @@
     upper_rows = lax.all_gather(top_local, "row", axis=1, tiled=True).reshape(PANEL_W, col_width)
     block_width = panel_lower.shape[1]
     empty_sum = jnp.zeros((row_count, col_width), jnp.float32)
-    shard_piece = lax.all_gather(panel_lower, "col", axis=1, tiled=True)
+    shard_piece = arrange_the_shifts_all(panel_lower)
     blocks_in = shard_piece.shape[1] // block_width
 
     def one_block(blocknum, running):

time: 445 us -> 561 us (1.26)
  the two profiles are of different devices: /device:TPU:8 before, /device:TPU:37 now
where the time goes in v1:
time: 561 us; the launch traced here: 559 us
  waiting for transfers between devices  414 us (74%)
  starting transfers between devices  35.6 us (6%)
  matrix products  33.4 us (6%)
  local copies, waits for them, and re-layouts  31.2 us (6%)
  blocking collectives  24.9 us (4%)
  between operations  13.5 us (2%)
  other arithmetic  5.61 us (1%)
    all_to_all x1, waiting for transfers between devices, divide_joints(): block_now = lax.all_to_all(carry_out, 'col', 0, 0)  313 us
    all_gather x1, waiting for transfers between devices, per_device(): lax.all_gather(top_local, 'row', axis=1, tiled=True)  66.8 us
    ppermute x2, waiting for transfers between devices, from_partner(): return lax.ppermute(block, axis, route)  34.2 us
    dot_general x16, matrix products, one_block(): product = jnp.dot(panel_part, rows_used, preferred_element_type=jnp.float32)  33.4 us
    ppermute x2, starting transfers between devices, from_partner(): return lax.ppermute(block, axis, route)  26.5 us
    all_to_all x1, blocking collectives, per_device(): lax.all_to_all(transformed.reshape(row_count // groups, groups, col_width...  24.9 us
    all_to_all x1, local copies, waits for them, and re-layouts, divide_joints(): block_now = lax.all_to_all(carry_out, 'col', 0, 0)  21.7 us
  transfers between devices with their start and end apart: 4, of which 4 were waited for; matrix products, arithmetic and copies ran while one was open for 1% of the time, Pallas kernels for 0%

profile of v1, /device:TPU:37, one launch (start us, length us, event | category | flops | bytes accessed | tf_op | source)
XLA Modules:
  0.0 558.9 jit_solution(11976034694853730466)
XLA Ops:
  6.5 0.7 convert_element_type.54
  7.2 1.4 multiply_convert_fusion
  8.6 10.6 %collective-permute-start = (bf16[2048,128]{1,0:T(8,128)(2,1)S(1)}, bf16[2048,128]{1,0:T(8,128)(2,1)S(1)}, u32[]{:S(2)}, u32[]{:S(2)}) collective-permute-start(bf16[2048,128]{1,0:T(8,128)(2,1)S(1)} %multiply_convert_fusion), channel_id=1, source_target_pairs={{0,256},{256,0},{16,272},{272,16},{32,288},{288,32},{48,304},{304,... | collective-permute-start | bytes 1572872 | tf_op jit(solution)/shard_map/ppermute | solution.py:27
  19.3 0.7 convert_element_type.53
  20.0 11.0 %collective-permute-done = bf16[2048,128]{1,0:T(8,128)(2,1)S(1)} collective-permute-done((bf16[2048,128]{1,0:T(8,128)(2,1)S(1)}, bf16[2048,128]{1,0:T(8,128)(2,1)S(1)}, u32[]{:S(2)}, u32[]{:S(2)}) %collective-permute-start) | collective-permute-done | bytes 524320 | tf_op jit(solution)/shard_map/ppermute | solution.py:27
  31.0 1.7 fusion.8
  32.7 15.9 %collective-permute-start.1 = (bf16[2048,128]{1,0:T(8,128)(2,1)S(1)}, bf16[2048,128]{1,0:T(8,128)(2,1)S(1)}, u32[]{:S(2)}, u32[]{:S(2)}) collective-permute-start(bf16[2048,128]{1,0:T(8,128)(2,1)S(1)} %fusion.8), channel_id=1, source_target_pairs={{0,128},{128,0},{16,144},{144,16},{32,160},{160,32},{48,176},{176,... | collective-permute-start | bytes 1572872 | tf_op jit(solution)/shard_map/ppermute | solution.py:27
  48.6 23.2 %collective-permute-done.1 = bf16[2048,128]{1,0:T(8,128)(2,1)S(1)} collective-permute-done((bf16[2048,128]{1,0:T(8,128)(2,1)S(1)}, bf16[2048,128]{1,0:T(8,128)(2,1)S(1)}, u32[]{:S(2)}, u32[]{:S(2)}) %collective-permute-start.1) | collective-permute-done | bytes 524320 | tf_op jit(solution)/shard_map/ppermute | solution.py:27
  71.7 0.3 fusion.12
  72.0 0.2 copy.8
  72.2 24.9 %all_to_all.20 = bf16[64,32,128]{2,0,1:T(8,128)(2,1)S(1)} all-to-all(bf16[64,32,128]{2,0,1:T(8,128)(2,1)S(1)} %copy.8), channel_id=1, replica_groups=mesh['row'=32,'col'=16] {'row'}, dimensions={1} | all-to-all | bytes 1048576 | tf_op jit(solution)/shard_map/all_to_all | solution.py:52
  97.2 6.8 %stack.2 = bf16[16,2048,256]{2,1,0:T(8,128)(2,1)} broadcast(bf16[2048,256]{1,0:T(8,128)(2,1)} %param.9), dimensions={1,2} | broadcast | bytes 17825792 | tf_op jit(solution)/shard_map/stack | solution.py:12
  103.9 9.1 %all-to-all-start.1 = ((bf16[16,2048,256]{2,1,0:T(8,128)(2,1)}), bf16[16,2048,256]{2,1,0:T(8,128)(2,1)}, u32[]{:S(2)}, u32[]{:S(2)}) async-start(bf16[16,2048,256]{2,1,0:T(8,128)(2,1)} %stack.2), calls=%async_computation.1 | async-start | bytes 33554432 | tf_op jit(solution)/shard_map/all_to_all | solution.py:13
  113.0 0.0 all-gather.2.cloned.1.call-start
  113.1 0.6 slice.5
  113.7 0.1 all-gather.2.cloned.1.call-update
  113.8 66.8 %all-gather.2.cloned.1.call-done = bf16[128,32,128]{2,0,1:T(8,128)(2,1)} async-done(((bf16[128,1,128]{2,0,1:T(8,128)(2,1)}), bf16[128,32,128]{2,0,1:T(8,128)(2,1)}) %all-gather.2.cloned.1.call-update) | async-done | bytes 1048592 | tf_op jit(solution)/shard_map/all_gather | solution.py:62
  180.6 1.9 copy.10
  182.5 313.2 %all-to-all-done.1 = bf16[16,2048,256]{2,1,0:T(8,128)(2,1)} async-done(((bf16[16,2048,256]{2,1,0:T(8,128)(2,1)}), bf16[16,2048,256]{2,1,0:T(8,128)(2,1)}, u32[]{:S(2)}, u32[]{:S(2)}) %all-to-all-start.1) | async-done | bytes 16777248 | tf_op jit(solution)/shard_map/all_to_all | solution.py:13
  495.7 21.7 %copy.9 = bf16[16,2048,256]{1,2,0:T(8,128)(2,1)} copy(bf16[16,2048,256]{2,1,0:T(8,128)(2,1)} %all-to-all-done.1) | data formatting | bytes 33554432 | tf_op jit(solution)/shard_map/all_to_all | solution.py:13
  517.3 33.8 %while.14 = (s32[]{:T(128)}, f32[2048,128]{1,0:T(8,128)S(1)}, bf16[2048,4096]{0,1:T(8,128)(2,1)}, bf16[4096,128]{1,0:T(8,128)(2,1)S(1)}, s32[]{:T(128)}, /*index=5*/s32[]{:T(128)}, s32[]{:T(128)}, s32[]{:T(128)}) while((s32[]{:T(128)}, f32[2048,128]{1,0:T(8,128)S(1)}, bf16[2048,4096]{0,1:T(8,128)(2,1)}, ...), condition=%wide.region_1.2_spmd.clone, body=%wide.region_0.1_spmd.clone.sunk | while | flops 135266304 | bytes 3212948 | solution.py:74
  517.3 2.1 fusion.20
  519.5 2.1 fusion.20
  521.6 2.1 fusion.20
  523.7 2.1 fusion.20
  525.8 2.1 fusion.20
  527.9 2.1 fusion.20
  530.0 2.1 fusion.20
  532.1 2.1 fusion.20
  534.3 2.1 fusion.20
  536.4 2.1 fusion.20
  538.5 2.1 fusion.20
  540.6 2.1 fusion.20
  542.7 2.1 fusion.20
  544.8 2.1 fusion.20
  546.9 2.1 fusion.20
  549.1 2.1 fusion.20
  551.2 0.9 fusion.14
  (1 shorter events, 0.0 us)
Async XLA Ops:
  8.6 22.4 %collective-permute-start = (bf16[2048,128]{1,0:T(8,128)(2,1)S(1)}, bf16[2048,128]{1,0:T(8,128)(2,1)S(1)}, u32[]{:S(2)}, u32[]{:S(2)}) collective-permute-start(bf16[2048,128]{1,0:T(8,128)(2,1)S(1)} %multiply_convert_fusion), channel_id=1, source_target_pairs={{0,256},{256,0},{16,272},{272,16},{32,288},{288,32},{48,304},{304,... | collective-permute-start | bytes 1572872 | tf_op jit(solution)/shard_map/ppermute | solution.py:27
  32.7 39.1 %collective-permute-start.1 = (bf16[2048,128]{1,0:T(8,128)(2,1)S(1)}, bf16[2048,128]{1,0:T(8,128)(2,1)S(1)}, u32[]{:S(2)}, u32[]{:S(2)}) collective-permute-start(bf16[2048,128]{1,0:T(8,128)(2,1)S(1)} %fusion.8), channel_id=1, source_target_pairs={{0,128},{128,0},{16,144},{144,16},{32,160},{160,32},{48,176},{176,... | collective-permute-start | bytes 1572872 | tf_op jit(solution)/shard_map/ppermute | solution.py:27
  103.9 391.7 %all-to-all-start.1 = ((bf16[16,2048,256]{2,1,0:T(8,128)(2,1)}), bf16[16,2048,256]{2,1,0:T(8,128)(2,1)}, u32[]{:S(2)}, u32[]{:S(2)}) async-start(bf16[16,2048,256]{2,1,0:T(8,128)(2,1)} %stack.2), calls=%async_computation.1 | async-start | bytes 33554432 | tf_op jit(solution)/shard_map/all_to_all | solution.py:13
  113.0 67.6 %all-gather.2.cloned.1.call-start = ((), (), s32[]{:S(2)}) async-start(), calls=%async_computation.2 | async-start | bytes 1081344 | tf_op jit(solution)/shard_map/all_gather | solution.py:62
Sparse Core Ops, SparseCore 0:
  116.0 64.5 all-gather.1
